TPU v7x, 256 devices: a whole 4x4x8 slice. The times are simulated.
256 devices in a mesh: dom: 256 (over y, x, z, core).
Axes of the slice: x: 4, y: 4, z: 8, core: 2. Of those that a mesh axis runs over, the one named last changes fastest.
Arguments:
- embeddings: float32 [131072, 400], P('dom'), may hold values from -1.8 to 1.8
- row_state: float32 [131072], P('dom'), may hold values from 0.01 to 1
- relations: float32 [2048, 400], P('dom'), may hold values from 0.5 to 1.5
- relation_state: float32 [2048], P('dom'), may hold values from 0.01 to 1
- partner_mask: int32 [1], replicated, may hold values from 1 to 255
- source_rows: int32 [786432], P('dom'), may hold values from 0 to 511
- relation_ids: int32 [786432], P('dom'), may hold values from 0 to 2047
- dest_rows: int32 [786432], P('dom'), may hold values from 0 to 511
- negative_rows: int32 [3072, 512], P('dom'), may hold values from 0 to 511
- edge_count: int32 [256], P('dom'), may hold values from 1 to 3072, 491520 in all
Outputs:
- new_embeddings: float32 [131072, 400], P('dom')
- new_row_state: float32 [131072], P('dom')
- new_relations: float32 [2048, 400], P('dom')
- new_relation_state: float32 [2048], P('dom')
Inputs may be any that keep to these rules, and one draw needn't show every extreme that they name: Device i trains the bucket of partition i with partition i XOR partner_mask[0]. `edge_count`: some bucket has all 3072 slots live.
All inputs are finite; a program needn't handle non-finite values. No bound on the sum of `edge_count` on one device may be relied on, other than what follows from the above.
Results may differ from a plain program's by a relative error of at most 0.0015.
Values may be sent and summed in bfloat16 or wider, within the bound.
No kernel may reach another device: no remote copies, remote signals or barrier semaphores. Data moves between devices by JAX's collectives and lax.ppermute only.
A program may use at most 128 MiB of HBM per device.

v0:
```python
import jax
import jax.numpy as jnp
from jax import lax
from jax.sharding import PartitionSpec as P


def from_partner(value, axis, bit):
    mask = 2**bit
    pairs = [(source, source ^ mask) for source in range(lax.axis_size(axis))]
    return lax.ppermute(value, axis, pairs)


def train_bucket(own_bf, part_bf, rel_bf, source, rel_ids, target_rows, negatives, live_count):
    groups, negs_per = negatives.shape
    edges = source.shape[0]
    group_len = edges // groups
    width = own_bf.shape[1]
    own_rows = own_bf[source].astype(jnp.float32)
    rel_rows = rel_bf[rel_ids].astype(jnp.float32)
    queries = (own_rows * rel_rows).astype(jnp.bfloat16)
    target_vals = part_bf[target_rows]
    positive = jnp.sum(queries.astype(jnp.float32) * target_vals.astype(jnp.float32), axis=1)
    sampled = part_bf[negatives]
    grouped = queries.reshape(groups, group_len, width)
    scores = jnp.einsum("gkd,gnd->gkn", grouped, sampled, preferred_element_type=jnp.float32)
    live = (jnp.arange(edges, dtype=jnp.int32) < live_count).astype(jnp.float32)
    pos_grad = -live * jax.nn.sigmoid(-positive)
    neg_grad = (live.reshape(groups, group_len, 1) * jax.nn.sigmoid(scores) / negs_per).astype(
        jnp.bfloat16
    )
    query_grad = pos_grad[:, None] * target_vals.astype(jnp.float32) + jnp.einsum(
        "gkn,gnd->gkd", neg_grad, sampled, preferred_element_type=jnp.float32
    ).reshape(edges, width)
    own_grad = (
        jnp.zeros((own_bf.shape[0], width), jnp.float32).at[source].add(query_grad * rel_rows)
    )
    rel_grad = (
        jnp.zeros((rel_bf.shape[0], width), jnp.float32).at[rel_ids].add(query_grad * own_rows)
    )
    neg_terms = jnp.einsum(
        "gkn,gkd->gnd", neg_grad, grouped, preferred_element_type=jnp.float32
    ).reshape(groups * negs_per, width)
    part_grad = (
        jnp.zeros((part_bf.shape[0], width), jnp.float32)
        .at[target_rows]
        .add(pos_grad[:, None] * queries.astype(jnp.float32))
    )
    part_grad = part_grad.at[negatives.reshape(-1)].add(neg_terms)
    return (own_grad, part_grad.astype(jnp.bfloat16), rel_grad)


def bit_is_set(partner_mask, bit_pos):
    return jnp.bitwise_and(jnp.right_shift(partner_mask[0], bit_pos), 1) == 1


def keep_value(value):
    return value


def swap_forward(bit_pos, value):
    return from_partner(value, "dom", bit_pos)


def swap_back(bit_pos, value):
    return from_partner(value, "dom", bit_pos)


def forward_at(bit_pos):

    def carry_over(value):
        return swap_forward(bit_pos, value)

    return carry_over


def backward_at(bit_pos):

    def carry_back(value):
        return swap_back(bit_pos, value)

    return carry_back


def local(
    embeddings,
    row_state,
    relations,
    relation_state,
    partner_mask,
    source_rows,
    relation_ids,
    dest_rows,
    negative_rows,
    edge_count,
):
    rel_bf = lax.all_gather(relations.astype(jnp.bfloat16), "dom", axis=0, tiled=True)
    own_bf = embeddings.astype(jnp.bfloat16)
    section_count = lax.axis_size("dom").bit_length() - 1
    section_bits = list(range(section_count))
    part_bf = own_bf
    for bit_pos in section_bits:
        part_bf = lax.cond(
            bit_is_set(partner_mask, bit_pos), forward_at(bit_pos), keep_value, part_bf
        )
    own_grad, part_grad, rel_grad = train_bucket(
        own_bf, part_bf, rel_bf, source_rows, relation_ids, dest_rows, negative_rows, edge_count[0]
    )
    returned = part_grad
    for bit_pos in section_bits:
        returned = lax.cond(
            bit_is_set(partner_mask, bit_pos), backward_at(bit_pos), keep_value, returned
        )
    grad = own_grad + returned.astype(jnp.float32)
    new_row_state = row_state + jnp.mean(grad * grad, axis=1)
    new_embeddings = embeddings - 0.1 * grad / jnp.sqrt(new_row_state)[:, None]
    rel_local = relations.shape[0]
    summed = lax.psum(rel_grad, "dom")
    rel_share = lax.dynamic_slice_in_dim(summed, lax.axis_index("dom") * rel_local, rel_local, 0)
    new_relation_state = relation_state + jnp.mean(rel_share * rel_share, axis=1)
    new_relations = relations - 0.1 * rel_share / jnp.sqrt(new_relation_state)[:, None]
    return (new_embeddings, new_row_state, new_relations, new_relation_state)


def solution(mesh):
    in_specs = (
        P("dom", None),
        P("dom"),
        P("dom", None),
        P("dom"),
        P(),
        P("dom"),
        P("dom"),
        P("dom"),
        P("dom", None),
        P("dom"),
    )
    out_specs = (P("dom", None), P("dom"), P("dom", None), P("dom"))
    return jax.shard_map(local, mesh=mesh, in_specs=in_specs, out_specs=out_specs, check_vma=False)
```

profile of v0, /device:TPU:2, one launch (start us, length us, event | category | flops | bytes accessed | tf_op | source)
XLA Modules:
  0.0 463.9 jit_solution(4562606726680797934)
XLA Ops:
  12.5 13.3 %gather_fusion = bf16[3072,400]{1,0:T(8,128)(2,1)} fusion(bf16[512,400]{1,0:T(8,128)(2,1)S(1)} %convert_element_type.144, s32[3072]{0:T(1024)S(1)} %get-tuple-element.107), kind=kCustom, calls=%fused_computation | custom fusion | bytes 4927488 | tf_op jit(solution)/shard_map/gather | solution.py:18
  25.8 27.7 %conditional.18 = (bf16[512,400]{1,0:T(8,128)(2,1)}) conditional(s32[]{:T(128)} %bitcast.5, bf16[512,400]{1,0:T(8,128)(2,1)} %get-tuple-element.111, bf16[512,400]{1,0:T(8,128)(2,1)} %get-tuple-element.111), branch_computations={%region_4.0_spmd, %region_5.0_spmd} | conditional | bytes 2457648 | solution.py:102
  25.9 3.4 collective-permute-start.2
  29.2 23.5 %collective-permute-done.2 = bf16[512,400]{1,0:T(8,128)(2,1)S(1)} collective-permute-done((bf16[512,400]{1,0:T(8,128)(2,1)}, bf16[512,400]{1,0:T(8,128)(2,1)S(1)}, u32[]{:S(2)}, u32[]{:S(2)}) %collective-permute-start.2) | collective-permute-done | bytes 409632 | tf_op jit(solution)/shard_map/cond/branch_1_fun/ppermute | solution.py:10
  53.5 15.6 %conditional.21 = (bf16[512,400]{1,0:T(8,128)(2,1)}) conditional(s32[]{:T(128)} %bitcast.2, bf16[512,400]{1,0:T(8,128)(2,1)} %get-tuple-element.114, bf16[512,400]{1,0:T(8,128)(2,1)} %get-tuple-element.114), branch_computations={%region_10.0_spmd, %region_11.0_spmd} | conditional | bytes 2457648 | solution.py:102
  53.5 2.1 collective-permute-start.5
  55.7 12.7 %collective-permute-done.5 = bf16[512,400]{1,0:T(8,128)(2,1)S(1)} collective-permute-done((bf16[512,400]{1,0:T(8,128)(2,1)}, bf16[512,400]{1,0:T(8,128)(2,1)S(1)}, u32[]{:S(2)}, u32[]{:S(2)}) %collective-permute-start.5) | collective-permute-done | bytes 409632 | tf_op jit(solution)/shard_map/cond/branch_1_fun/ppermute | solution.py:10
  69.2 15.1 %conditional.23 = (bf16[512,400]{1,0:T(8,128)(2,1)}) conditional(s32[]{:T(128)} %bitcast, bf16[512,400]{1,0:T(8,128)(2,1)} %get-tuple-element.116, bf16[512,400]{1,0:T(8,128)(2,1)} %get-tuple-element.116), branch_computations={%region_14.0_spmd, %region_15.0_spmd} | conditional | bytes 2457648 | solution.py:102
  69.2 3.2 collective-permute-start.7
  72.3 11.1 %collective-permute-done.7 = bf16[512,400]{1,0:T(8,128)(2,1)S(1)} collective-permute-done((bf16[512,400]{1,0:T(8,128)(2,1)}, bf16[512,400]{1,0:T(8,128)(2,1)S(1)}, u32[]{:S(2)}, u32[]{:S(2)}) %collective-permute-start.7) | collective-permute-done | bytes 409632 | tf_op jit(solution)/shard_map/cond/branch_1_fun/ppermute | solution.py:10
  84.3 14.5 %gather_fusion.2 = bf16[3072,400]{1,0:T(8,128)(2,1)} fusion(bf16[512,400]{1,0:T(8,128)(2,1)} %get-tuple-element.117, s32[3072]{0:T(1024)S(1)} %get-tuple-element.108), kind=kCustom, calls=%fused_computation.2 | custom fusion | bytes 4927488 | tf_op jit(solution)/shard_map/gather | solution.py:21
  98.8 26.9 %gather_fusion.3 = bf16[6144,400]{1,0:T(8,128)(2,1)} fusion(bf16[512,400]{1,0:T(8,128)(2,1)} %get-tuple-element.117, s32[6144]{0:T(1024)S(1)} %broadcast_clamp_fusion), kind=kCustom, calls=%fused_computation.3 | custom fusion | bytes 9854976 | tf_op jit(solution)/shard_map/gather | solution.py:23
  126.4 3.1 all-gather.2.cloned.1.call-done
  129.5 13.0 %gather_fusion.1 = bf16[3072,400]{1,0:T(8,128)(2,1)S(1)} fusion(bf16[2048,400]{1,0:T(8,128)(2,1)} %all-gather.2.cloned.1.call-done, s32[3072]{0:T(1024)S(1)} %get-tuple-element.105), kind=kCustom, calls=%fused_computation.1 | custom fusion | bytes 4927488 | tf_op jit(solution)/shard_map/gather | solution.py:19
  142.6 5.5 %fusion.4 = (f32[3072]{0:T(1024)S(1)}, bf16[3072,400]{1,0:T(8,128)(2,1)S(1)}) fusion(bf16[3072,400]{1,0:T(8,128)(2,1)} %gather_fusion.2, bf16[3072,400]{1,0:T(8,128)(2,1)S(1)} %gather_fusion.1, bf16[3072,400]{1,0:T(8,128)(2,1)} %gather_fusion), kind=kLoop, calls=%fused_computation.18 | loop fusion | flops 9827328 | bytes 9842688 | tf_op jit(solution)/shard_map/reduce_sum | solution.py:22
  148.4 2.3 multiply_convert_fusion
  153.8 3.3 fusion.5
  157.0 22.0 %scatter_custom_fusion.3 = f32[2048,400]{1,0:T(8,128)} fusion(s32[3072]{0:T(1024)S(1)} %get-tuple-element.104, f32[3072,400]{1,0:T(8,128)} %fusion.5, bf16[3072,400]{1,0:T(8,128)(2,1)S(1)} %copy-done.4, f32[]{:T(128)} %constant.66.clone.1), kind=kCustom, calls=%fused_computation.14 | custom fusion | flops 3686400 | bytes 11337732 | tf_op jit(solution)/shard_map/scatter-add | solution.py:38
  179.1 20.9 %scatter_custom_fusion = f32[512,400]{1,0:T(8,128)S(1)} fusion(s32[3072]{0:T(1024)S(1)} %get-tuple-element.109, bf16[3072,400]{1,0:T(8,128)(2,1)} %copy-done.1, f32[3072]{0:T(1024)S(1)} %divide_multiply_fusion, f32[]{:T(128)} %constant.66.clone.1), kind=kCustom, calls=%fused_computation.17 | custom fusion | flops 3686400 | bytes 3289092 | tf_op jit(solution)/shard_map/scatter-add | solution.py:46
  200.0 9.3 %fusion.13 = f32[12,512,400]{2,1,0:T(8,128)} fusion(bf16[12,256,512]{2,1,0:T(8,128)(2,1)} %copy-done.6, bf16[12,256,400]{2,1,0:T(8,128)(2,1)} %bitcast.31), kind=kOutput, calls=%fused_computation.45 | convolution fusion | flops 1258291200 | bytes 15433728 | tf_op jit(solution)/shard_map/reshape | solution.py:42
  209.3 37.5 %scatter_fusion = f32[512,400]{1,0:T(8,128)S(1)} fusion(f32[512,400]{1,0:T(8,128)S(1)} %scatter_custom_fusion, s32[6144]{0:T(1024)S(1)} %bitcast.34, f32[6144,400]{1,0:T(8,128)} %bitcast.27), kind=kCustom, calls=%fused_computation.5 | custom fusion | flops 2457600 | bytes 29515776 | tf_op jit(solution)/shard_map/scatter-add | solution.py:48
  247.7 28.1 %conditional.26 = (bf16[512,400]{1,0:T(8,128)(2,1)}) conditional(s32[]{:T(128)} %bitcast.5, bf16[512,400]{1,0:T(8,128)(2,1)} %get-tuple-element.119, bf16[512,400]{1,0:T(8,128)(2,1)} %get-tuple-element.119), branch_computations={%region_23.0_spmd, %region_24.0_spmd} | conditional | bytes 2457648 | solution.py:110
  249.7 25.3 %collective-permute-done.10 = bf16[512,400]{1,0:T(8,128)(2,1)S(1)} collective-permute-done((bf16[512,400]{1,0:T(8,128)(2,1)}, bf16[512,400]{1,0:T(8,128)(2,1)S(1)}, u32[]{:S(2)}, u32[]{:S(2)}) %collective-permute-start.10) | collective-permute-done | bytes 409632 | tf_op jit(solution)/shard_map/cond/branch_1_fun/ppermute | solution.py:10
  275.8 15.7 %conditional.29 = (bf16[512,400]{1,0:T(8,128)(2,1)}) conditional(s32[]{:T(128)} %bitcast.2, bf16[512,400]{1,0:T(8,128)(2,1)} %get-tuple-element.122, bf16[512,400]{1,0:T(8,128)(2,1)} %get-tuple-element.122), branch_computations={%region_29.0_spmd, %region_30.0_spmd} | conditional | bytes 2457648 | solution.py:110
  275.8 2.1 collective-permute-start.13
  277.9 12.8 %collective-permute-done.13 = bf16[512,400]{1,0:T(8,128)(2,1)S(1)} collective-permute-done((bf16[512,400]{1,0:T(8,128)(2,1)}, bf16[512,400]{1,0:T(8,128)(2,1)S(1)}, u32[]{:S(2)}, u32[]{:S(2)}) %collective-permute-start.13) | collective-permute-done | bytes 409632 | tf_op jit(solution)/shard_map/cond/branch_1_fun/ppermute | solution.py:10
  291.5 15.0 %conditional.31 = (bf16[512,400]{1,0:T(8,128)(2,1)}) conditional(s32[]{:T(128)} %bitcast, bf16[512,400]{1,0:T(8,128)(2,1)} %get-tuple-element.124, bf16[512,400]{1,0:T(8,128)(2,1)} %get-tuple-element.124), branch_computations={%region_33.0_spmd, %region_34.0_spmd} | conditional | bytes 2457648 | solution.py:110
  291.5 2.8 collective-permute-start.15
  294.3 11.4 %collective-permute-done.15 = bf16[512,400]{1,0:T(8,128)(2,1)S(1)} collective-permute-done((bf16[512,400]{1,0:T(8,128)(2,1)}, bf16[512,400]{1,0:T(8,128)(2,1)S(1)}, u32[]{:S(2)}, u32[]{:S(2)}) %collective-permute-start.15) | collective-permute-done | bytes 409632 | tf_op jit(solution)/shard_map/cond/branch_1_fun/ppermute | solution.py:10
  306.5 2.2 convert_element_type.155
  308.7 21.9 %scatter_custom_fusion.2 = f32[512,400]{1,0:T(8,128)} fusion(f32[512,400]{1,0:T(8,128)} %convert_element_type.155, s32[3072]{0:T(1024)S(1)} %get-tuple-element.106, f32[3072,400]{1,0:T(8,128)} %fusion.5, bf16[3072,400]{1,0:T(8,128)(2,1)S(1)} %copy-done.3), kind=kCustom, calls=%fused_computation.16 | custom fusion | flops 3686400 | bytes 10256384 | tf_op jit(solution)/shard_map/scatter-add | solution.py:35
  335.5 118.7 %all-reduce.2.cloned.1.call-done = f32[2048,400]{1,0:T(8,128)} async-done(((f32[2048,400]{1,0:T(8,128)}), f32[2048,400]{1,0:T(8,128)}) %all-reduce.2.cloned.1.call-update) | async-done | bytes 3276816 | tf_op jit(solution)/shard_map/psum | solution.py:117
  (72 shorter events, 24.4 us)
Async XLA Ops:
  7.2 122.4 %all-gather.2.cloned.1.call-start = ((), (), s32[]{:S(2)}) async-start(), calls=%async_computation | async-start | bytes 2105344 | tf_op jit(solution)/shard_map/all_gather | solution.py:96
  8.6 445.7 %all-reduce.2.cloned.1.call-start = ((), (), s32[]{:S(2)}) async-start(), calls=%async_computation.1 | async-start | bytes 8388608 | tf_op jit(solution)/shard_map/psum | solution.py:117
  10.7 15.1 %copy-start.7 = (f32[512,400]{1,0:T(8,128)}, f32[512,400]{1,0:T(8,128)S(1)}, u32[]{:S(2)}) copy-start(f32[512,400]{1,0:T(8,128)S(1)} %copy.39) | copy-start | bytes 2457604
  12.5 13.3 %copy-start.8 = (s32[12,512]{1,0:T(8,128)S(1)}, s32[12,512]{1,0:T(8,128)}, u32[]{:S(2)}) copy-start(s32[12,512]{1,0:T(8,128)} %param.50) | copy-start | bytes 73732
  25.8 58.5 %copy-start.10 = (s32[3072]{0:T(1024)S(1)}, s32[3072]{0:T(1024)}, u32[]{:S(2)}) copy-start(s32[3072]{0:T(1024)} %param.49) | copy-start | bytes 36868
  25.9 26.9 %collective-permute-start.2 = (bf16[512,400]{1,0:T(8,128)(2,1)}, bf16[512,400]{1,0:T(8,128)(2,1)S(1)}, u32[]{:S(2)}, u32[]{:S(2)}) collective-permute-start(bf16[512,400]{1,0:T(8,128)(2,1)} %param.5), channel_id=1, source_target_pairs={{0,4},{1,5},{2,6},{3,7},{4,0},{5,1},{6,2},{7,3},{8,12},{9,13},{10,... | collective-permute-start | bytes 1228808 | tf_op jit(solution)/shard_map/cond/branch_1_fun/ppermute | solution.py:10
  53.5 14.8 %collective-permute-start.5 = (bf16[512,400]{1,0:T(8,128)(2,1)}, bf16[512,400]{1,0:T(8,128)(2,1)S(1)}, u32[]{:S(2)}, u32[]{:S(2)}) collective-permute-start(bf16[512,400]{1,0:T(8,128)(2,1)} %param.11), channel_id=1, source_target_pairs={{0,32},{1,33},{2,34},{3,35},{4,36},{5,37},{6,38},{7,39},{8,40},{9,... | collective-permute-start | bytes 1228808 | tf_op jit(solution)/shard_map/cond/branch_1_fun/ppermute | solution.py:10
  69.2 14.3 %collective-permute-start.7 = (bf16[512,400]{1,0:T(8,128)(2,1)}, bf16[512,400]{1,0:T(8,128)(2,1)S(1)}, u32[]{:S(2)}, u32[]{:S(2)}) collective-permute-start(bf16[512,400]{1,0:T(8,128)(2,1)} %param.15), channel_id=1, source_target_pairs={{0,128},{1,129},{2,130},{3,131},{4,132},{5,133},{6,134},{7,135},{8... | collective-permute-start | bytes 1228808 | tf_op jit(solution)/shard_map/cond/branch_1_fun/ppermute | solution.py:10
  98.8 27.6 %copy-start.11 = (s32[3072]{0:T(1024)S(1)}, s32[3072]{0:T(1024)}, u32[]{:S(2)}) copy-start(s32[3072]{0:T(1024)} %param.48) | copy-start | bytes 36868
  142.6 5.5 %copy-start.2 = (bf16[3072,400]{1,0:T(8,128)(2,1)}, bf16[3072,400]{1,0:T(8,128)(2,1)S(1)}, u32[]{:S(2)}) copy-start(bf16[3072,400]{1,0:T(8,128)(2,1)S(1)} %gather_fusion.1) | copy-start | bytes 7372804
  142.6 5.8 %copy-start = (bf16[6144,400]{1,0:T(8,128)(2,1)S(1)}, bf16[6144,400]{1,0:T(8,128)(2,1)}, u32[]{:S(2)}) copy-start(bf16[6144,400]{1,0:T(8,128)(2,1)} %gather_fusion.3) | copy-start | bytes 14745604
  148.1 2.6 copy-start.1
  150.7 1.8 copy-start.6
  150.7 3.0 copy-start.5
  153.8 3.3 copy-start.4
  247.7 61.0 %copy-start.3 = (bf16[3072,400]{1,0:T(8,128)(2,1)S(1)}, bf16[3072,400]{1,0:T(8,128)(2,1)}, u32[]{:S(2)}) copy-start(bf16[3072,400]{1,0:T(8,128)(2,1)} %copy-done.2) | copy-start | bytes 7372804
  247.7 27.3 %collective-permute-start.10 = (bf16[512,400]{1,0:T(8,128)(2,1)}, bf16[512,400]{1,0:T(8,128)(2,1)S(1)}, u32[]{:S(2)}, u32[]{:S(2)}) collective-permute-start(bf16[512,400]{1,0:T(8,128)(2,1)} %param.21), channel_id=1, source_target_pairs={{0,4},{1,5},{2,6},{3,7},{4,0},{5,1},{6,2},{7,3},{8,12},{9,13},{10,... | collective-permute-start | bytes 1228808 | tf_op jit(solution)/shard_map/cond/branch_1_fun/ppermute | solution.py:10
  275.8 14.9 %collective-permute-start.13 = (bf16[512,400]{1,0:T(8,128)(2,1)}, bf16[512,400]{1,0:T(8,128)(2,1)S(1)}, u32[]{:S(2)}, u32[]{:S(2)}) collective-permute-start(bf16[512,400]{1,0:T(8,128)(2,1)} %param.27), channel_id=1, source_target_pairs={{0,32},{1,33},{2,34},{3,35},{4,36},{5,37},{6,38},{7,39},{8,40},{9,... | collective-permute-start | bytes 1228808 | tf_op jit(solution)/shard_map/cond/branch_1_fun/ppermute | solution.py:10
  291.5 14.2 %collective-permute-start.15 = (bf16[512,400]{1,0:T(8,128)(2,1)}, bf16[512,400]{1,0:T(8,128)(2,1)S(1)}, u32[]{:S(2)}, u32[]{:S(2)}) collective-permute-start(bf16[512,400]{1,0:T(8,128)(2,1)} %param.31), channel_id=1, source_target_pairs={{0,128},{1,129},{2,130},{3,131},{4,132},{5,133},{6,134},{7,135},{8... | collective-permute-start | bytes 1228808 | tf_op jit(solution)/shard_map/cond/branch_1_fun/ppermute | solution.py:10
  306.5 25.5 %copy-start.12 = (f32[512]{0:T(512)S(1)}, f32[512]{0:T(512)}, u32[]{:S(2)}) copy-start(f32[512]{0:T(512)} %param.43) | copy-start | bytes 6148
  308.7 146.4 %copy-start.13 = (f32[8]{0:T(128)S(1)}, f32[8]{0:T(128)}, u32[]{:S(2)}) copy-start(f32[8]{0:T(128)} %param.45) | copy-start | bytes 100
  308.7 146.9 %copy-start.9 = (f32[8,400]{1,0:T(8,128)S(1)}, f32[8,400]{1,0:T(8,128)}, u32[]{:S(2)}) copy-start(f32[8,400]{1,0:T(8,128)} %param.44) | copy-start | bytes 38404
Sparse Core Ops, SparseCore 0:
  12.3 117.2 all-gather.1
  179.2 275.0 all-reduce.1
where the time goes:
time: 465 us; the launch traced here: 464 us
  waiting for transfers between devices  219 us (47%)
  other arithmetic  123 us (26%)
  local copies, waits for them, and re-layouts  77.7 us (17%)
  starting transfers between devices  15.7 us (3%)
  between operations  15.6 us (3%)
  matrix products  13.4 us (3%)
    psum x1, waiting for transfers between devices, local(): summed = lax.psum(rel_grad, 'dom')  119 us
    ppermute x6, waiting for transfers between devices, from_partner(): return lax.ppermute(value, axis, pairs)  96.8 us
    scatter-add x1, other arithmetic, train_bucket(): part_grad = part_grad.at[negatives.reshape(-1)].add(neg_terms)  37.5 us
    gather x1, local copies, waits for them, and re-layouts, train_bucket(): sampled = part_bf[negatives]  26.9 us
    scatter-add x1, other arithmetic, train_bucket(): jnp.zeros((rel_bf.shape[0], width), jnp.float32).at[rel_ids]  22 us
    scatter-add x1, other arithmetic, train_bucket(): jnp.zeros((own_bf.shape[0], width), jnp.float32).at[source]  21.9 us
    scatter-add x1, other arithmetic, train_bucket(): part_grad = jnp.zeros((part_bf.shape[0], width), jnp.float32).at[target_r...  20.9 us
    ppermute x6, starting transfers between devices, from_partner(): return lax.ppermute(value, axis, pairs)  15.6 us
  transfers between devices with their start and end apart: 8, of which 8 were waited for; matrix products, arithmetic and copies ran while one was open for 35% of the time, Pallas kernels for 0%

commit v1 on v0

--- a/solution.py
+++ b/solution.py
@@ -93,7 +93,12 @@
     negative_rows,
     edge_count,
 ):
-    rel_bf = lax.all_gather(relations.astype(jnp.bfloat16), "dom", axis=0, tiled=True)
+    rel_bf = jnp.concatenate(
+        lax.all_to_all(
+            jnp.stack([relations.astype(jnp.bfloat16)] * lax.axis_size("dom")), "dom", 0, 0
+        ),
+        axis=0,
+    )
     own_bf = embeddings.astype(jnp.bfloat16)
     section_count = lax.axis_size("dom").bit_length() - 1
     section_bits = list(range(section_count))

time: 465 us -> 500 us (1.075)
  waiting for transfers between devices: 219 us -> 241 us
  starting transfers between devices: 15.7 us -> 28.2 us
    ppermute x6, waiting for transfers between devices: 96.8 us -> 123 us  [from_partner(): return lax.ppermute(value, axis, pairs)]
    all_to_all x0 -> x1, starting transfers between devices: none -> 14.7 us  [local(): lax.all_to_all(jnp.stack([relations.astype(jnp.bfloat16)] * lax.axis_size...]
  transfers between devices with their start and end apart: 8 -> 8, of which waited for: 8 -> 7; matrix products, arithmetic and copies ran while one was open for 35% -> 32% of each run, Pallas kernels for 0% -> 0%
where the time goes in v1:
time: 500 us
  waiting for transfers between devices  241 us (48%)
  other arithmetic  123 us (25%)
  local copies, waits for them, and re-layouts  78.8 us (16%)
  starting transfers between devices  28.2 us (6%)
  between operations  15.6 us (3%)
  matrix products  13.4 us (3%)
    ppermute x6, waiting for transfers between devices, from_partner(): return lax.ppermute(value, axis, pairs)  123 us
    psum x1, waiting for transfers between devices, local(): summed = lax.psum(rel_grad, 'dom')  118 us
    scatter-add x1, other arithmetic, train_bucket(): part_grad = part_grad.at[negatives.reshape(-1)].add(neg_terms)  37.5 us
    gather x1, local copies, waits for them, and re-layouts, train_bucket(): sampled = part_bf[negatives]  26.8 us
    scatter-add x1, other arithmetic, train_bucket(): jnp.zeros((rel_bf.shape[0], width), jnp.float32).at[rel_ids]  22 us
    scatter-add x1, other arithmetic, train_bucket(): jnp.zeros((own_bf.shape[0], width), jnp.float32).at[source]  21.9 us
    scatter-add x1, other arithmetic, train_bucket(): part_grad = jnp.zeros((part_bf.shape[0], width), jnp.float32).at[target_r...  20.9 us
    all_to_all x1, starting transfers between devices, local(): lax.all_to_all(jnp.stack([relations.astype(jnp.bfloat16)] * lax.axis_size...  14.7 us
  transfers between devices with their start and end apart: 8, of which 7 were waited for; matrix products, arithmetic and copies ran while one was open for 32% of the time, Pallas kernels for 0%

profile of v1, /device:TPU:2, one launch (start us, length us, event | category | flops | bytes accessed | tf_op | source)
XLA Modules:
  0.0 499.6 jit_solution(1691882036540403006)
XLA Ops:
  9.4 14.7 %all-to-all-start = ((bf16[256,8,400]{2,1,0:T(8,128)(2,1)}), bf16[256,8,400]{2,1,0:T(8,128)(2,1)S(1)}, u32[]{:S(2)}, u32[]{:S(2)}) async-start(bf16[256,8,400]{2,1,0:T(8,128)(2,1)} %stack.2), calls=%async_computation | async-start | bytes 4194304 | tf_op jit(solution)/shard_map/all_to_all | solution.py:97
  28.3 13.3 %gather_fusion = bf16[3072,400]{1,0:T(8,128)(2,1)} fusion(bf16[512,400]{1,0:T(8,128)(2,1)S(1)} %convert_element_type.144, s32[3072]{0:T(1024)S(1)} %get-tuple-element.107), kind=kCustom, calls=%fused_computation | custom fusion | bytes 4927488 | tf_op jit(solution)/shard_map/gather | solution.py:18
  41.6 52.8 %conditional.18 = (bf16[512,400]{1,0:T(8,128)(2,1)}) conditional(s32[]{:T(128)} %bitcast.5, bf16[512,400]{1,0:T(8,128)(2,1)} %get-tuple-element.111, bf16[512,400]{1,0:T(8,128)(2,1)} %get-tuple-element.111), branch_computations={%region_4.0_spmd, %region_5.0_spmd} | conditional | bytes 2457648 | solution.py:107
  41.6 2.9 collective-permute-start.2
  44.5 49.1 %collective-permute-done.2 = bf16[512,400]{1,0:T(8,128)(2,1)S(1)} collective-permute-done((bf16[512,400]{1,0:T(8,128)(2,1)}, bf16[512,400]{1,0:T(8,128)(2,1)S(1)}, u32[]{:S(2)}, u32[]{:S(2)}) %collective-permute-start.2) | collective-permute-done | bytes 409632 | tf_op jit(solution)/shard_map/cond/branch_1_fun/ppermute | solution.py:10
  94.4 15.9 %conditional.21 = (bf16[512,400]{1,0:T(8,128)(2,1)}) conditional(s32[]{:T(128)} %bitcast.2, bf16[512,400]{1,0:T(8,128)(2,1)} %get-tuple-element.114, bf16[512,400]{1,0:T(8,128)(2,1)} %get-tuple-element.114), branch_computations={%region_10.0_spmd, %region_11.0_spmd} | conditional | bytes 2457648 | solution.py:107
  94.4 2.1 collective-permute-start.5
  96.5 13.0 %collective-permute-done.5 = bf16[512,400]{1,0:T(8,128)(2,1)S(1)} collective-permute-done((bf16[512,400]{1,0:T(8,128)(2,1)}, bf16[512,400]{1,0:T(8,128)(2,1)S(1)}, u32[]{:S(2)}, u32[]{:S(2)}) %collective-permute-start.5) | collective-permute-done | bytes 409632 | tf_op jit(solution)/shard_map/cond/branch_1_fun/ppermute | solution.py:10
  110.3 15.1 %conditional.23 = (bf16[512,400]{1,0:T(8,128)(2,1)}) conditional(s32[]{:T(128)} %bitcast, bf16[512,400]{1,0:T(8,128)(2,1)} %get-tuple-element.116, bf16[512,400]{1,0:T(8,128)(2,1)} %get-tuple-element.116), branch_computations={%region_14.0_spmd, %region_15.0_spmd} | conditional | bytes 2457648 | solution.py:107
  110.3 3.1 collective-permute-start.7
  113.4 11.1 %collective-permute-done.7 = bf16[512,400]{1,0:T(8,128)(2,1)S(1)} collective-permute-done((bf16[512,400]{1,0:T(8,128)(2,1)}, bf16[512,400]{1,0:T(8,128)(2,1)S(1)}, u32[]{:S(2)}, u32[]{:S(2)}) %collective-permute-start.7) | collective-permute-done | bytes 409632 | tf_op jit(solution)/shard_map/cond/branch_1_fun/ppermute | solution.py:10
  125.4 14.4 %gather_fusion.2 = bf16[3072,400]{1,0:T(8,128)(2,1)} fusion(bf16[512,400]{1,0:T(8,128)(2,1)} %get-tuple-element.117, s32[3072]{0:T(1024)S(1)} %get-tuple-element.108), kind=kCustom, calls=%fused_computation.2 | custom fusion | bytes 4927488 | tf_op jit(solution)/shard_map/gather | solution.py:21
  139.9 26.8 %gather_fusion.3 = bf16[6144,400]{1,0:T(8,128)(2,1)} fusion(bf16[512,400]{1,0:T(8,128)(2,1)} %get-tuple-element.117, s32[6144]{0:T(1024)S(1)} %broadcast_clamp_fusion), kind=kCustom, calls=%fused_computation.3 | custom fusion | bytes 9854976 | tf_op jit(solution)/shard_map/gather | solution.py:23
  167.4 13.2 %gather_fusion.1 = bf16[3072,400]{1,0:T(8,128)(2,1)} fusion(bf16[2048,400]{1,0:T(8,128)(2,1)S(1)} %bitcast.28, s32[3072]{0:T(1024)S(1)} %get-tuple-element.105), kind=kCustom, calls=%fused_computation.1 | custom fusion | bytes 4927488 | tf_op jit(solution)/shard_map/gather | solution.py:19
  180.6 5.3 %fusion.4 = (f32[3072]{0:T(1024)S(1)}, bf16[3072,400]{1,0:T(8,128)(2,1)S(1)}) fusion(bf16[3072,400]{1,0:T(8,128)(2,1)} %gather_fusion.2, bf16[3072,400]{1,0:T(8,128)(2,1)} %gather_fusion.1, bf16[3072,400]{1,0:T(8,128)(2,1)} %gather_fusion), kind=kLoop, calls=%fused_computation.18 | loop fusion | flops 9827328 | bytes 9842688 | tf_op jit(solution)/shard_map/reduce_sum | solution.py:22
  186.1 2.3 multiply_convert_fusion
  191.5 3.3 fusion.5
  194.8 22.0 %scatter_custom_fusion.3 = f32[2048,400]{1,0:T(8,128)} fusion(s32[3072]{0:T(1024)S(1)} %get-tuple-element.104, f32[3072,400]{1,0:T(8,128)} %fusion.5, bf16[3072,400]{1,0:T(8,128)(2,1)S(1)} %copy-done.3, f32[]{:T(128)} %constant.66.clone.1), kind=kCustom, calls=%fused_computation.14 | custom fusion | flops 3686400 | bytes 11337732 | tf_op jit(solution)/shard_map/scatter-add | solution.py:38
  216.9 20.9 %scatter_custom_fusion = f32[512,400]{1,0:T(8,128)S(1)} fusion(s32[3072]{0:T(1024)S(1)} %get-tuple-element.109, bf16[3072,400]{1,0:T(8,128)(2,1)} %copy-done.1, f32[3072]{0:T(1024)S(1)} %divide_multiply_fusion, f32[]{:T(128)} %constant.66.clone.1), kind=kCustom, calls=%fused_computation.17 | custom fusion | flops 3686400 | bytes 3289092 | tf_op jit(solution)/shard_map/scatter-add | solution.py:46
  237.8 9.3 %fusion.13 = f32[12,512,400]{2,1,0:T(8,128)} fusion(bf16[12,256,512]{2,1,0:T(8,128)(2,1)} %copy-done.5, bf16[12,256,400]{2,1,0:T(8,128)(2,1)} %bitcast.33), kind=kOutput, calls=%fused_computation.45 | convolution fusion | flops 1258291200 | bytes 15433728 | tf_op jit(solution)/shard_map/reshape | solution.py:42
  247.0 37.5 %scatter_fusion = f32[512,400]{1,0:T(8,128)S(1)} fusion(f32[512,400]{1,0:T(8,128)S(1)} %scatter_custom_fusion, s32[6144]{0:T(1024)S(1)} %bitcast.36, f32[6144,400]{1,0:T(8,128)} %bitcast.29), kind=kCustom, calls=%fused_computation.5 | custom fusion | flops 2457600 | bytes 29515776 | tf_op jit(solution)/shard_map/scatter-add | solution.py:48
  285.5 25.3 %conditional.26 = (bf16[512,400]{1,0:T(8,128)(2,1)}) conditional(s32[]{:T(128)} %bitcast.5, bf16[512,400]{1,0:T(8,128)(2,1)} %get-tuple-element.119, bf16[512,400]{1,0:T(8,128)(2,1)} %get-tuple-element.119), branch_computations={%region_23.0_spmd, %region_24.0_spmd} | conditional | bytes 2457648 | solution.py:115
  285.5 24.5 %collective-permute-done.10 = bf16[512,400]{1,0:T(8,128)(2,1)S(1)} collective-permute-done((bf16[512,400]{1,0:T(8,128)(2,1)}, bf16[512,400]{1,0:T(8,128)(2,1)S(1)}, u32[]{:S(2)}, u32[]{:S(2)}) %collective-permute-start.10) | collective-permute-done | bytes 409632 | tf_op jit(solution)/shard_map/cond/branch_1_fun/ppermute | solution.py:10
  310.8 16.4 %conditional.29 = (bf16[512,400]{1,0:T(8,128)(2,1)}) conditional(s32[]{:T(128)} %bitcast.2, bf16[512,400]{1,0:T(8,128)(2,1)} %get-tuple-element.122, bf16[512,400]{1,0:T(8,128)(2,1)} %get-tuple-element.122), branch_computations={%region_29.0_spmd, %region_30.0_spmd} | conditional | bytes 2457648 | solution.py:115
  310.8 2.2 collective-permute-start.13
  313.0 13.4 %collective-permute-done.13 = bf16[512,400]{1,0:T(8,128)(2,1)S(1)} collective-permute-done((bf16[512,400]{1,0:T(8,128)(2,1)}, bf16[512,400]{1,0:T(8,128)(2,1)S(1)}, u32[]{:S(2)}, u32[]{:S(2)}) %collective-permute-start.13) | collective-permute-done | bytes 409632 | tf_op jit(solution)/shard_map/cond/branch_1_fun/ppermute | solution.py:10
  327.1 15.7 %conditional.31 = (bf16[512,400]{1,0:T(8,128)(2,1)}) conditional(s32[]{:T(128)} %bitcast, bf16[512,400]{1,0:T(8,128)(2,1)} %get-tuple-element.124, bf16[512,400]{1,0:T(8,128)(2,1)} %get-tuple-element.124), branch_computations={%region_33.0_spmd, %region_34.0_spmd} | conditional | bytes 2457648 | solution.py:115
  327.1 3.2 collective-permute-start.15
  330.3 11.7 %collective-permute-done.15 = bf16[512,400]{1,0:T(8,128)(2,1)S(1)} collective-permute-done((bf16[512,400]{1,0:T(8,128)(2,1)}, bf16[512,400]{1,0:T(8,128)(2,1)S(1)}, u32[]{:S(2)}, u32[]{:S(2)}) %collective-permute-start.15) | collective-permute-done | bytes 409632 | tf_op jit(solution)/shard_map/cond/branch_1_fun/ppermute | solution.py:10
  342.8 2.2 convert_element_type.155
  345.0 21.9 %scatter_custom_fusion.2 = f32[512,400]{1,0:T(8,128)} fusion(f32[512,400]{1,0:T(8,128)} %convert_element_type.155, s32[3072]{0:T(1024)S(1)} %get-tuple-element.106, f32[3072,400]{1,0:T(8,128)} %fusion.5, bf16[3072,400]{1,0:T(8,128)(2,1)S(1)} %copy-done.2), kind=kCustom, calls=%fused_computation.16 | custom fusion | flops 3686400 | bytes 10256384 | tf_op jit(solution)/shard_map/scatter-add | solution.py:35
  371.8 118.1 %all-reduce.2.cloned.1.call-done = f32[2048,400]{1,0:T(8,128)} async-done(((f32[2048,400]{1,0:T(8,128)}), f32[2048,400]{1,0:T(8,128)}) %all-reduce.2.cloned.1.call-update) | async-done | bytes 3276816 | tf_op jit(solution)/shard_map/psum | solution.py:122
  (72 shorter events, 23.3 us)
Async XLA Ops:
  7.2 17.7 %copy-start.6 = (f32[512,400]{0,1:T(8,128)S(1)}, f32[512,400]{0,1:T(8,128)}, u32[]{:S(2)}) copy-start(f32[512,400]{0,1:T(8,128)} %param.42) | copy-start | bytes 2457604
  7.2 21.1 %copy-start.9 = (s32[3072]{0:T(1024)S(1)}, s32[3072]{0:T(1024)}, u32[]{:S(2)}) copy-start(s32[3072]{0:T(1024)} %param.47) | copy-start | bytes 36868
  9.4 157.9 %all-to-all-start = ((bf16[256,8,400]{2,1,0:T(8,128)(2,1)}), bf16[256,8,400]{2,1,0:T(8,128)(2,1)S(1)}, u32[]{:S(2)}, u32[]{:S(2)}) async-start(bf16[256,8,400]{2,1,0:T(8,128)(2,1)} %stack.2), calls=%async_computation | async-start | bytes 4194304 | tf_op jit(solution)/shard_map/all_to_all | solution.py:97
  24.1 465.8 %all-reduce.2.cloned.1.call-start = ((), (), s32[]{:S(2)}) async-start(), calls=%async_computation.1 | async-start | bytes 8388608 | tf_op jit(solution)/shard_map/psum | solution.py:122
  28.3 13.3 %copy-start.7 = (s32[12,512]{1,0:T(8,128)S(1)}, s32[12,512]{1,0:T(8,128)}, u32[]{:S(2)}) copy-start(s32[12,512]{1,0:T(8,128)} %param.50) | copy-start | bytes 73732
  41.6 83.8 %copy-start.10 = (s32[3072]{0:T(1024)S(1)}, s32[3072]{0:T(1024)}, u32[]{:S(2)}) copy-start(s32[3072]{0:T(1024)} %param.49) | copy-start | bytes 36868
  41.6 52.0 %collective-permute-start.2 = (bf16[512,400]{1,0:T(8,128)(2,1)}, bf16[512,400]{1,0:T(8,128)(2,1)S(1)}, u32[]{:S(2)}, u32[]{:S(2)}) collective-permute-start(bf16[512,400]{1,0:T(8,128)(2,1)} %param.5), channel_id=1, source_target_pairs={{0,4},{1,5},{2,6},{3,7},{4,0},{5,1},{6,2},{7,3},{8,12},{9,13},{10,... | collective-permute-start | bytes 1228808 | tf_op jit(solution)/shard_map/cond/branch_1_fun/ppermute | solution.py:10
  94.4 15.1 %collective-permute-start.5 = (bf16[512,400]{1,0:T(8,128)(2,1)}, bf16[512,400]{1,0:T(8,128)(2,1)S(1)}, u32[]{:S(2)}, u32[]{:S(2)}) collective-permute-start(bf16[512,400]{1,0:T(8,128)(2,1)} %param.11), channel_id=1, source_target_pairs={{0,32},{1,33},{2,34},{3,35},{4,36},{5,37},{6,38},{7,39},{8,40},{9,... | collective-permute-start | bytes 1228808 | tf_op jit(solution)/shard_map/cond/branch_1_fun/ppermute | solution.py:10
  110.3 14.2 %collective-permute-start.7 = (bf16[512,400]{1,0:T(8,128)(2,1)}, bf16[512,400]{1,0:T(8,128)(2,1)S(1)}, u32[]{:S(2)}, u32[]{:S(2)}) collective-permute-start(bf16[512,400]{1,0:T(8,128)(2,1)} %param.15), channel_id=1, source_target_pairs={{0,128},{1,129},{2,130},{3,131},{4,132},{5,133},{6,134},{7,135},{8... | collective-permute-start | bytes 1228808 | tf_op jit(solution)/shard_map/cond/branch_1_fun/ppermute | solution.py:10
  139.9 27.5 %copy-start.11 = (s32[3072]{0:T(1024)S(1)}, s32[3072]{0:T(1024)}, u32[]{:S(2)}) copy-start(s32[3072]{0:T(1024)} %param.48) | copy-start | bytes 36868
  180.6 5.5 %copy-start = (bf16[6144,400]{1,0:T(8,128)(2,1)S(1)}, bf16[6144,400]{1,0:T(8,128)(2,1)}, u32[]{:S(2)}) copy-start(bf16[6144,400]{1,0:T(8,128)(2,1)} %gather_fusion.3) | copy-start | bytes 14745604
  185.9 2.5 copy-start.1
  188.5 1.8 copy-start.5
  188.5 3.0 copy-start.4
  191.5 3.3 copy-start.3
  285.4 59.5 %copy-start.2 = (bf16[3072,400]{1,0:T(8,128)(2,1)S(1)}, bf16[3072,400]{1,0:T(8,128)(2,1)}, u32[]{:S(2)}) copy-start(bf16[3072,400]{1,0:T(8,128)(2,1)} %gather_fusion.1) | copy-start | bytes 7372804
  285.5 24.5 %collective-permute-start.10 = (bf16[512,400]{1,0:T(8,128)(2,1)}, bf16[512,400]{1,0:T(8,128)(2,1)S(1)}, u32[]{:S(2)}, u32[]{:S(2)}) collective-permute-start(bf16[512,400]{1,0:T(8,128)(2,1)} %param.21), channel_id=1, source_target_pairs={{0,4},{1,5},{2,6},{3,7},{4,0},{5,1},{6,2},{7,3},{8,12},{9,13},{10,... | collective-permute-start | bytes 1228808 | tf_op jit(solution)/shard_map/cond/branch_1_fun/ppermute | solution.py:10
  310.8 15.6 %collective-permute-start.13 = (bf16[512,400]{1,0:T(8,128)(2,1)}, bf16[512,400]{1,0:T(8,128)(2,1)S(1)}, u32[]{:S(2)}, u32[]{:S(2)}) collective-permute-start(bf16[512,400]{1,0:T(8,128)(2,1)} %param.27), channel_id=1, source_target_pairs={{0,32},{1,33},{2,34},{3,35},{4,36},{5,37},{6,38},{7,39},{8,40},{9,... | collective-permute-start | bytes 1228808 | tf_op jit(solution)/shard_map/cond/branch_1_fun/ppermute | solution.py:10
  327.1 14.9 %collective-permute-start.15 = (bf16[512,400]{1,0:T(8,128)(2,1)}, bf16[512,400]{1,0:T(8,128)(2,1)S(1)}, u32[]{:S(2)}, u32[]{:S(2)}) collective-permute-start(bf16[512,400]{1,0:T(8,128)(2,1)} %param.31), channel_id=1, source_target_pairs={{0,128},{1,129},{2,130},{3,131},{4,132},{5,133},{6,134},{7,135},{8... | collective-permute-start | bytes 1228808 | tf_op jit(solution)/shard_map/cond/branch_1_fun/ppermute | solution.py:10
  342.8 25.5 %copy-start.12 = (f32[512]{0:T(512)S(1)}, f32[512]{0:T(512)}, u32[]{:S(2)}) copy-start(f32[512]{0:T(512)} %param.43) | copy-start | bytes 6148
  345.0 145.8 %copy-start.13 = (f32[8]{0:T(128)S(1)}, f32[8]{0:T(128)}, u32[]{:S(2)}) copy-start(f32[8]{0:T(128)} %param.45) | copy-start | bytes 100
  345.0 146.3 %copy-start.8 = (f32[8,400]{1,0:T(8,128)S(1)}, f32[8,400]{1,0:T(8,128)}, u32[]{:S(2)}) copy-start(f32[8,400]{1,0:T(8,128)} %param.44) | copy-start | bytes 38404
Sparse Core Ops, SparseCore 0:
  216.9 272.9 all-reduce.1
